TPU v7x, 512 devices: a whole 4x4x16 slice. The times are simulated.
512 devices in a mesh: lat: 16 (over z_hi, y), lon: 32 (over z_lo, x, core).
Axes of the slice: x: 4, y: 4, z: 16 (z_hi: 4, z_lo: 4; z = z_hi * 4 + z_lo), core: 2. Of those that a mesh axis runs over, the one named last changes fastest.
Arguments:
- queries: float32 [64, 1024, 512], P('lat', 'lon'), may hold values from -80 to 80
- key_rows: float32 [512, 512], P(('lat', 'lon')), may hold values from -8 to 8
- value_rows: float32 [512, 512], P(('lat', 'lon')), may hold values from -6 to 6
- cotangent: float32 [64, 1024, 512], P('lat', 'lon'), may hold values from -25 to 25
- conv_taps: float32 [9, 512], replicated, may hold values from -1.75 to 1.75
Outputs:
- query_grad: float32 [64, 1024, 512], P('lat', 'lon')
- key_grad: float32 [512, 512], P(('lat', 'lon'))
- value_grad: float32 [512, 512], P(('lat', 'lon'))
- tap_update: float32 [9, 512], replicated
All inputs are finite; a program needn't handle non-finite values.
Results may differ from a plain program's by a relative error of at most 0.0003.
Values sent between devices are 32-bit elements; how exact they have to be, the bound alone decides.
A program may use at most 64 MiB of HBM per device.

v0:
```python
import jax
import jax.numpy as jnp
from jax import lax
from jax.sharding import PartitionSpec as P

HD = 64
HIGH = lax.Precision.HIGHEST
OFFSETS = ((-1, -1), (-1, 0), (-1, 1), (0, -1), (0, 0), (0, 1), (1, -1), (1, 0), (1, 1))


def joined_along(pieces, dim):
    lengths = list(pieces.shape[1:])
    lengths[dim] *= pieces.shape[0]
    return jnp.moveaxis(pieces, 0, dim).reshape(lengths)


def copy_for_each(value, axis):
    copies = jnp.broadcast_to(value, (lax.axis_size(axis), *value.shape))
    return lax.all_to_all(copies, axis, split_axis=0, concat_axis=0, tiled=True)


def gather_directly(value, axis, dim):
    return joined_along(copy_for_each(value, axis), dim)


def extended(value, sides, width):
    for axis, dim in sides:
        peers, length = (lax.axis_size(axis), value.shape[dim])
        up = [(i, (i + 1) % peers) for i in range(peers)]
        down = [(j, i) for i, j in up]
        last = lax.slice_in_dim(value, length - width, length, axis=dim)
        initial = lax.slice_in_dim(value, 0, width, axis=dim)
        before = lax.ppermute(last, axis, up)
        after = lax.ppermute(initial, axis, down)
        value = jnp.concatenate([before, value, after], axis=dim)
    return value


def cut_along(value, dim, peers):
    lengths = value.shape
    pieces = value.reshape(*lengths[:dim], peers, lengths[dim] // peers, *lengths[dim + 1 :])
    return jnp.moveaxis(pieces, dim, 0)


def summed_on_arrival(value, axis, dim):
    peers = lax.axis_size(axis)
    pieces = lax.all_to_all(cut_along(value, dim, peers), axis, 0, 0, tiled=True)
    return jnp.sum(pieces, axis=0)


def split_heads(matrix):
    return matrix.reshape(matrix.shape[0], -1, HD)


def latitude_weights(row_count, band_index, band_count):
    line_total = row_count * band_count
    centres = (jnp.arange(line_total, dtype=jnp.float32) + 0.5) * (jnp.pi / line_total)
    mean_cosine = jnp.sum(jnp.sin(centres)) / line_total
    mine = (band_index * row_count + jnp.arange(row_count, dtype=jnp.int32)).astype(jnp.float32)
    return jnp.sin((mine + 0.5) * (jnp.pi / line_total)) / mean_cosine


def close_poles(padded, row_dim, band_index, band_count):
    height = padded.shape[row_dim]
    positions = jnp.arange(height)
    outside = (positions == 0) & (band_index == 0) | (positions == height - 1) & (
        band_index == band_count - 1
    )
    shape_mask = [1] * padded.ndim
    shape_mask[row_dim] = height
    return jnp.where(outside.reshape(shape_mask), 0.0, padded)


def spread_taps(weighted, grad_padded, conv_taps):
    row_count, col_count = (weighted.shape[0], weighted.shape[1])
    result = weighted
    for tap_index, (shift_row, shift_col) in enumerate(OFFSETS):
        result = (
            result
            + conv_taps[tap_index]
            * grad_padded[
                1 - shift_row : 1 - shift_row + row_count, 1 - shift_col : 1 - shift_col + col_count
            ]
        )
    return result


def tap_terms(weighted, out_padded):
    row_count, col_count = (weighted.shape[0], weighted.shape[1])
    term_list = []
    for shift_row, shift_col in OFFSETS:
        term_list.append(
            jnp.sum(
                out_padded[
                    1 + shift_row : 1 + shift_row + row_count,
                    1 + shift_col : 1 + shift_col + col_count,
                ]
                * weighted,
                axis=(0, 1),
            )
        )
    return jnp.stack(term_list)


def group_logits(query_part, key_part):
    return jnp.einsum(
        "qhd,khd->hqk", split_heads(query_part), split_heads(key_part), precision=HIGH
    ) * HD ** (-0.5)


def body(queries, key_rows, value_rows, cotangent, conv_taps):
    row_count, col_count, channels = queries.shape
    band_count = lax.axis_size("lat")
    band_index = lax.axis_index("lat")
    weighted = cotangent * latitude_weights(row_count, band_index, band_count)[:, None, None]
    paired_rows = jnp.concatenate([key_rows, value_rows], 1)
    paired_sector = gather_directly(paired_rows, "lon", 0)
    paired_all = lax.all_gather(paired_sector, "lat", axis=0, tiled=True)
    key_all = paired_all[:, :channels]
    value_all = paired_all[:, channels:]
    token_count = row_count * col_count
    key_count = key_all.shape[0]
    query_flat = queries.reshape(token_count, channels)
    group_width = 2 * HD
    group_count = channels // group_width
    outputs = []
    peaks = []
    sums_soft = []
    for group_index in range(group_count):
        col_start = group_index * group_width
        col_stop = col_start + group_width
        logits = group_logits(query_flat[:, col_start:col_stop], key_all[:, col_start:col_stop])
        row_peak = jnp.max(logits, -1, keepdims=True)
        raised = jnp.exp(logits - row_peak)
        normaliser = jnp.sum(raised, -1, keepdims=True)
        soft_weights = raised / normaliser
        outputs.append(
            jnp.einsum(
                "hqk,khd->qhd",
                soft_weights,
                split_heads(value_all[:, col_start:col_stop]),
                precision=HIGH,
            ).reshape(token_count, group_width)
        )
        peaks.append(row_peak)
        sums_soft.append(normaliser)
    out_flat = jnp.concatenate(outputs, 1)
    out_grid = out_flat.reshape(row_count, col_count, channels)
    both_padded = close_poles(
        extended(jnp.stack([weighted, out_grid]), (("lat", 1), ("lon", 2)), 1),
        1,
        band_index,
        band_count,
    )
    grad_padded = both_padded[0]
    out_padded = both_padded[1]
    out_grad = spread_taps(weighted, grad_padded, conv_taps)
    tap_sum = lax.psum(tap_terms(weighted, out_padded), ("lat", "lon"))
    tap_update = tap_sum / jnp.sqrt(jnp.mean(tap_sum * tap_sum) + 1e-06)
    grad_flat = out_grad.reshape(token_count, channels)
    query_parts = []
    key_parts = []
    value_parts = []
    for group_index in range(group_count):
        col_start = group_index * group_width
        col_stop = col_start + group_width
        query_heads = split_heads(query_flat[:, col_start:col_stop])
        key_heads = split_heads(key_all[:, col_start:col_stop])
        logits = jnp.einsum("qhd,khd->hqk", query_heads, key_heads, precision=HIGH) * HD ** (-0.5)
        soft_weights = jnp.exp(logits - peaks[group_index]) / sums_soft[group_index]
        grad_heads = split_heads(grad_flat[:, col_start:col_stop])
        value_parts.append(
            jnp.einsum("hqk,qhd->khd", soft_weights, grad_heads, precision=HIGH).reshape(
                key_count, group_width
            )
        )
        prob_grad = jnp.einsum(
            "qhd,khd->hqk",
            grad_heads,
            split_heads(value_all[:, col_start:col_stop]),
            precision=HIGH,
        )
        row_dot = jnp.transpose(
            jnp.sum(grad_heads * split_heads(out_flat[:, col_start:col_stop]), -1)
        )[:, :, None]
        logit_grad = soft_weights * (prob_grad - row_dot)
        query_parts.append(
            (
                jnp.einsum("hqk,khd->qhd", logit_grad, key_heads, precision=HIGH) * HD ** (-0.5)
            ).reshape(token_count, group_width)
        )
        key_parts.append(
            (
                jnp.einsum("hqk,qhd->khd", logit_grad, query_heads, precision=HIGH) * HD ** (-0.5)
            ).reshape(key_count, group_width)
        )
    paired_terms = jnp.concatenate(key_parts + value_parts, 1)
    paired_band = lax.psum_scatter(paired_terms, "lat", scatter_dimension=0, tiled=True)
    paired_grad = summed_on_arrival(paired_band, "lon", 0)
    key_grad = paired_grad[:, :channels]
    value_grad = paired_grad[:, channels:]
    query_grad = jnp.concatenate(query_parts, 1).reshape(row_count, col_count, channels)
    return (query_grad, key_grad, value_grad, tap_update)


def solution(mesh):
    placed = (
        P("lat", "lon", None),
        P(("lat", "lon"), None),
        P(("lat", "lon"), None),
        P("lat", "lon", None),
        P(),
    )
    return jax.shard_map(
        body,
        mesh=mesh,
        in_specs=placed,
        out_specs=(P("lat", "lon", None), P(("lat", "lon"), None), P(("lat", "lon"), None), P()),
        check_vma=False,
    )
```

profile of v0, /device:TPU:1, one launch (start us, length us, event | category | flops | bytes accessed | tf_op | source)
XLA Modules:
  0.0 343.2 jit_solution(12765066276765064027)
XLA Ops:
  8.0 18.8 %all_to_all.10 = f32[32,1,1024]{2,1,0:T(1,128)} all-to-all(f32[32,1,1024]{2,1,0:T(1,128)S(1)} %broadcast_in_dim.10), channel_id=1, replica_groups=mesh['lat'=16,'lon'=32] {'lon'}, dimensions={0} | all-to-all | bytes 262144 | tf_op jit(solution)/shard_map/all_to_all | solution.py:19
  30.8 1.0 fusion.50
  31.8 88.1 %all-gather.3.cloned.1.call-done = f32[512,1,1024]{2,1,0:T(1,128)} async-done(((f32[32,1,1024]{2,1,0:T(1,128)}), f32[512,1,1024]{2,1,0:T(1,128)}) %all-gather.3.cloned.1.call-update) | async-done | bytes 2097168 | tf_op jit(solution)/shard_map/all_gather | solution.py:118
  120.0 2.1 copy.158
  126.7 1.0 fusion.58
  127.8 1.1 convolution_bitcast_fusion.2
  133.1 1.4 convolution_bitcast_fusion.3
  134.8 2.1 collective-permute-start
  136.9 9.2 %collective-permute-start.1 = (f32[2,1,32,512]{3,2,1,0:T(8,128)S(1)}, f32[2,1,32,512]{3,2,1,0:T(8,128)S(1)}, u32[]{:S(2)}, u32[]{:S(2)}) collective-permute-start(f32[2,1,32,512]{3,2,1,0:T(8,128)S(1)} %get-tuple-element.26), channel_id=1, source_target_pairs={{32,0},{64,32},{96,64},{128,96},{160,128},{192,160},{224,192},{256... | collective-permute-start | bytes 393224 | tf_op jit(solution)/shard_map/ppermute | solution.py:34
  146.1 4.7 %collective-permute-done = f32[2,1,32,512]{3,2,1,0:T(8,128)S(1)} collective-permute-done((f32[2,1,32,512]{3,2,1,0:T(8,128)S(1)}, f32[2,1,32,512]{3,2,1,0:T(8,128)S(1)}, u32[]{:S(2)}, u32[]{:S(2)}) %collective-permute-start) | collective-permute-done | bytes 131104 | tf_op jit(solution)/shard_map/ppermute | solution.py:33
  150.9 3.2 collective-permute-start.2
  154.1 2.1 collective-permute-start.3
  156.3 3.3 collective-permute-done.3
  160.9 1.6 copy.153
  163.3 1.6 copy.155
  165.8 1.6 copy.154
  168.2 1.6 copy.156
  170.8 1.6 fusion.38
  181.8 1.9 copy.146
  184.1 117.4 %psum.7 = f32[9,512]{1,0:T(8,128)S(1)} all-reduce(f32[9,512]{1,0:T(8,128)S(1)} %stack.47), channel_id=1, replica_groups=mesh['lat'=16,'lon'=32] {'lat','lon'}, use_global_device_ids=true, to_apply=%region_24.25 | all-reduce | flops 4608 | bytes 36864 | tf_op jit(solution)/shard_map/psum | solution.py:158
  304.9 13.6 %reduce-scatter.4.cloned.1.call-done = f32[32,1024]{1,0:T(8,128)} async-done(((f32[512,1024]{1,0:T(8,128)}), f32[32,1024]{1,0:T(8,128)}) %reduce-scatter.4.cloned.1.call-update) | async-done | bytes 131088
  318.5 1.1 copy.147
  320.4 6.7 %all-to-all-start.1 = ((f32[32,1,1024]{2,1,0:T(1,128)}), f32[32,1,1024]{2,1,0:T(1,128)S(1)}, u32[]{:S(2)}, u32[]{:S(2)}) async-start(f32[32,1,1024]{2,1,0:T(1,128)} %copy.125), calls=%async_computation.1 | async-start | bytes 262144 | tf_op jit(solution)/shard_map/all_to_all | solution.py:47
  329.2 6.5 %all-to-all-done.1 = f32[32,1,1024]{2,1,0:T(1,128)S(1)} async-done(((f32[32,1,1024]{2,1,0:T(1,128)}), f32[32,1,1024]{2,1,0:T(1,128)S(1)}, u32[]{:S(2)}, u32[]{:S(2)}) %all-to-all-start.1) | async-done | bytes 131104 | tf_op jit(solution)/shard_map/all_to_all | solution.py:47
  (162 shorter events, 33.8 us)
Async XLA Ops:
  7.2 112.8 %all-gather.3.cloned.1.call-start = ((), (), s32[]{:S(2)}) async-start(), calls=%async_computation.3 | async-start | bytes 2228224 | tf_op jit(solution)/shard_map/all_gather | solution.py:118
  26.8 291.7 %reduce-scatter.4.cloned.1.call-start = ((), (), s32[]{:S(2)}) async-start(), calls=%async_computation.4 | async-start | bytes 2228224
  29.4 95.3 %copy-start.17 = (f32[128,128]{0,1:T(8,128)}, f32[128,128]{0,1:T(8,128)S(1)}, u32[]{:S(2)}) copy-start(f32[128,128]{0,1:T(8,128)S(1)} %copy.152) | copy-start | bytes 196612
  122.6 3.8 %copy-start.28 = (f32[512,128]{0,1:T(8,128)}, f32[512,128]{0,1:T(8,128)S(1)}, u32[]{:S(2)}) copy-start(f32[512,128]{0,1:T(8,128)S(1)} %copy.96) | copy-start | bytes 786436
  123.9 3.9 %copy-start.26 = (f32[512,128]{0,1:T(8,128)}, f32[512,128]{0,1:T(8,128)S(1)}, u32[]{:S(2)}) copy-start(f32[512,128]{0,1:T(8,128)S(1)} %copy.86) | copy-start | bytes 786436
  126.4 3.6 %copy-start.19 = (f32[128,2,64]{0,2,1:T(8,128)}, f32[128,2,64]{0,2,1:T(8,128)S(1)}, u32[]{:S(2)}) copy-start(f32[128,2,64]{0,2,1:T(8,128)S(1)} %convolution_bitcast_fusion) | copy-start | bytes 196612
  126.4 3.6 %copy-start.13 = (f32[128,128]{0,1:T(8,128)S(1)}, f32[128,128]{0,1:T(8,128)}, u32[]{:S(2)}) copy-start(f32[128,128]{0,1:T(8,128)} %copy.151) | copy-start | bytes 196612
  127.7 3.4 %copy-start.24 = (f32[512,128]{0,1:T(8,128)S(1)}, f32[512,128]{0,1:T(8,128)}, u32[]{:S(2)}) copy-start(f32[512,128]{0,1:T(8,128)} %copy.91) | copy-start | bytes 786436
  131.7 19.2 %copy-start.21 = (f32[128,2,64]{0,2,1:T(8,128)}, f32[128,2,64]{0,2,1:T(8,128)S(1)}, u32[]{:S(2)}) copy-start(f32[128,2,64]{0,2,1:T(8,128)S(1)} %convolution_bitcast_fusion.1) | copy-start | bytes 196612
  132.9 13.2 %copy-start.34 = (f32[9,512]{1,0:T(8,128)S(1)}, f32[9,512]{1,0:T(8,128)}, u32[]{:S(2)}) copy-start(f32[9,512]{1,0:T(8,128)} %param.9) | copy-start | bytes 55300
  134.5 16.3 %copy-start.22 = (f32[128,2,64]{0,2,1:T(8,128)}, f32[128,2,64]{0,2,1:T(8,128)S(1)}, u32[]{:S(2)}) copy-start(f32[128,2,64]{0,2,1:T(8,128)S(1)} %convolution_bitcast_fusion.3) | copy-start | bytes 196612
  134.8 16.0 %collective-permute-start = (f32[2,1,32,512]{3,2,1,0:T(8,128)S(1)}, f32[2,1,32,512]{3,2,1,0:T(8,128)S(1)}, u32[]{:S(2)}, u32[]{:S(2)}) collective-permute-start(f32[2,1,32,512]{3,2,1,0:T(8,128)S(1)} %get-tuple-element.25), channel_id=1, source_target_pairs={{0,32},{32,64},{64,96},{96,128},{128,160},{160,192},{192,224},{224... | collective-permute-start | bytes 393224 | tf_op jit(solution)/shard_map/ppermute | solution.py:33
  136.9 13.9 %collective-permute-start.1 = (f32[2,1,32,512]{3,2,1,0:T(8,128)S(1)}, f32[2,1,32,512]{3,2,1,0:T(8,128)S(1)}, u32[]{:S(2)}, u32[]{:S(2)}) collective-permute-start(f32[2,1,32,512]{3,2,1,0:T(8,128)S(1)} %get-tuple-element.26), channel_id=1, source_target_pairs={{32,0},{64,32},{96,64},{128,96},{160,128},{192,160},{224,192},{256... | collective-permute-start | bytes 393224 | tf_op jit(solution)/shard_map/ppermute | solution.py:34
  150.9 9.0 %copy-start = (f32[4,32,512]{2,1,0:T(8,128)S(1)}, f32[4,32,512]{2,1,0:T(8,128)}, u32[]{:S(2)}) copy-start(f32[4,32,512]{2,1,0:T(8,128)} %param.8) | copy-start | bytes 786436
  150.9 5.4 %collective-permute-start.2 = (f32[2,6,1,512]{3,2,1,0:T(1,128)S(1)}, f32[2,6,1,512]{3,2,1,0:T(1,128)S(1)}, u32[]{:S(2)}, u32[]{:S(2)}) collective-permute-start(f32[2,6,1,512]{3,2,1,0:T(1,128)S(1)} %get-tuple-element.23), channel_id=1, source_target_pairs={{0,1},{1,2},{2,3},{3,4},{4,5},{5,6},{6,7},{7,8},{8,9},{9,10},{10,1... | collective-permute-start | bytes 73736 | tf_op jit(solution)/shard_map/ppermute | solution.py:33
  154.1 5.4 %collective-permute-start.3 = (f32[2,6,1,512]{3,2,1,0:T(1,128)S(1)}, f32[2,6,1,512]{3,2,1,0:T(1,128)S(1)}, u32[]{:S(2)}, u32[]{:S(2)}) collective-permute-start(f32[2,6,1,512]{3,2,1,0:T(1,128)S(1)} %get-tuple-element.24), channel_id=1, source_target_pairs={{1,0},{2,1},{3,2},{4,3},{5,4},{6,5},{7,6},{8,7},{9,8},{10,9},{11,1... | collective-permute-start | bytes 73736 | tf_op jit(solution)/shard_map/ppermute | solution.py:34
  159.9 9.9 %copy-start.20 = (f32[128,2,64]{0,2,1:T(8,128)S(1)}, f32[128,2,64]{0,2,1:T(8,128)}, u32[]{:S(2)}) copy-start(f32[128,2,64]{0,2,1:T(8,128)} %copy-done.19) | copy-start | bytes 196612
  183.7 119.1 %copy-start.2 = (f32[512,128]{0,1:T(8,128)S(1)}, f32[512,128]{0,1:T(8,128)}, u32[]{:S(2)}) copy-start(f32[512,128]{0,1:T(8,128)} %copy-done.1) | copy-start | bytes 786436
  183.7 119.1 %copy-start.8 = (f32[2,128,512]{1,2,0:T(8,128)S(1)}, f32[2,128,512]{1,2,0:T(8,128)}, u32[]{:S(2)}) copy-start(f32[2,128,512]{1,2,0:T(8,128)} %copy-done.7) | copy-start | bytes 1572868
  183.7 119.8 %copy-start.4 = (f32[512,128]{0,1:T(8,128)S(1)}, f32[512,128]{0,1:T(8,128)}, u32[]{:S(2)}) copy-start(f32[512,128]{0,1:T(8,128)} %copy-done.3) | copy-start | bytes 786436
  183.7 119.8 %copy-start.10 = (f32[2,128,512]{1,2,0:T(8,128)S(1)}, f32[2,128,512]{1,2,0:T(8,128)}, u32[]{:S(2)}) copy-start(f32[2,128,512]{1,2,0:T(8,128)} %copy-done.9) | copy-start | bytes 1572868
  183.7 120.5 %copy-start.12 = (f32[2,128,512]{1,2,0:T(8,128)S(1)}, f32[2,128,512]{1,2,0:T(8,128)}, u32[]{:S(2)}) copy-start(f32[2,128,512]{1,2,0:T(8,128)} %copy-done.11) | copy-start | bytes 1572868
  303.4 23.7 %copy-start.6 = (f32[2,128,512]{1,2,0:T(8,128)S(1)}, f32[2,128,512]{1,2,0:T(8,128)}, u32[]{:S(2)}) copy-start(f32[2,128,512]{1,2,0:T(8,128)} %copy-done.5) | copy-start | bytes 1572868
  320.4 15.2 %all-to-all-start.1 = ((f32[32,1,1024]{2,1,0:T(1,128)}), f32[32,1,1024]{2,1,0:T(1,128)S(1)}, u32[]{:S(2)}, u32[]{:S(2)}) async-start(f32[32,1,1024]{2,1,0:T(1,128)} %copy.125), calls=%async_computation.1 | async-start | bytes 262144 | tf_op jit(solution)/shard_map/all_to_all | solution.py:47
  (18 other events, 43.5 us)
Sparse Core Ops, SparseCore 0:
  26.9 93.0 all-gather.2
  183.8 134.6 reduce-scatter.3
where the time goes:
time: 344 us; the launch traced here: 343 us
  blocking collectives  136 us (40%)
  waiting for transfers between devices  116 us (34%)
  starting transfers between devices  23.4 us (7%)
  local copies, waits for them, and re-layouts  21.9 us (6%)
  matrix products  19.9 us (6%)
  between operations  16.2 us (5%)
  other arithmetic  9.35 us (3%)
    psum x1, blocking collectives, body(): tap_sum = lax.psum(tap_terms(weighted, out_padded), ('lat', 'lon'))  117 us
    all_gather x1, waiting for transfers between devices, body(): paired_all = lax.all_gather(paired_sector, 'lat', axis=0, tiled=True)  88.1 us
    all_to_all x1, blocking collectives, copy_for_each(): return lax.all_to_all(copies, axis, split_axis=0, concat_axis=0, tiled=True)  18.8 us
    unnamed x3, waiting for transfers between devices  13.6 us
    unnamed x88, local copies, waits for them, and re-layouts  13.2 us
    ppermute x2, starting transfers between devices, extended(): after = lax.ppermute(initial, axis, down)  11.3 us
  transfers between devices with their start and end apart: 7, of which 5 were waited for; matrix products, arithmetic and copies ran while one was open for 3% of the time, Pallas kernels for 0%

commit v1 on v0

--- a/solution.py
+++ b/solution.py
@@ -115,7 +115,8 @@
     weighted = cotangent * latitude_weights(row_count, band_index, band_count)[:, None, None]
     paired_rows = jnp.concatenate([key_rows, value_rows], 1)
     paired_sector = gather_directly(paired_rows, "lon", 0)
-    paired_all = lax.all_gather(paired_sector, "lat", axis=0, tiled=True)
+    sent = jnp.stack([paired_sector] * lax.axis_size("lat"))
+    paired_all = jnp.concatenate(lax.all_to_all(sent, "lat", 0, 0), axis=0)
     key_all = paired_all[:, :channels]
     value_all = paired_all[:, channels:]
     token_count = row_count * col_count

time: 344 us -> 359 us (1.044)
  starting transfers between devices: 23.4 us -> 39 us
  blocking collectives: 136 us -> 141 us
  other arithmetic: 9.35 us -> 4.88 us
  local copies, waits for them, and re-layouts: 21.9 us -> 18.3 us
    all_to_all x0 -> x1, waiting for transfers between devices: none -> 93.8 us  [body(): paired_all = jnp.concatenate(lax.all_to_all(sent, 'lat', 0, 0), axis=0)]
    all_gather x1 -> x0, waiting for transfers between devices: 88.1 us -> none  [body(): paired_all = lax.all_gather(paired_sector, 'lat', axis=0, tiled=True)]
    all_to_all x0 -> x1, starting transfers between devices: none -> 15 us  [body(): paired_all = jnp.concatenate(lax.all_to_all(sent, 'lat', 0, 0), axis=0)]
    unnamed x88 -> x108, local copies, waits for them, and re-layouts: 13.2 us -> 6.39 us
    psum x1, blocking collectives: 117 us -> 123 us  [body(): tap_sum = lax.psum(tap_terms(weighted, out_padded), ('lat', 'lon'))]
    ppermute x2, waiting for transfers between devices: 4.69 us -> 0.81 us  [extended(): before = lax.ppermute(last, axis, up)]
    unnamed x3 -> x2, waiting for transfers between devices: 13.6 us -> 11.9 us
  transfers between devices with their start and end apart: 7 -> 7, of which waited for: 5 -> 6; matrix products, arithmetic and copies ran while one was open for 3% -> 2% of each run, Pallas kernels for 0% -> 0%
where the time goes in v1:
time: 359 us
  blocking collectives  141 us (39%)
  waiting for transfers between devices  117 us (33%)
  starting transfers between devices  39 us (11%)
  matrix products  21.3 us (6%)
  local copies, waits for them, and re-layouts  18.3 us (5%)
  between operations  16.4 us (5%)
  other arithmetic  4.88 us (1%)
    psum x1, blocking collectives, body(): tap_sum = lax.psum(tap_terms(weighted, out_padded), ('lat', 'lon'))  123 us
    all_to_all x1, waiting for transfers between devices, body(): paired_all = jnp.concatenate(lax.all_to_all(sent, 'lat', 0, 0), axis=0)  93.8 us
    all_to_all x1, blocking collectives, copy_for_each(): return lax.all_to_all(copies, axis, split_axis=0, concat_axis=0, tiled=True)  18.3 us
    all_to_all x1, starting transfers between devices, body(): paired_all = jnp.concatenate(lax.all_to_all(sent, 'lat', 0, 0), axis=0)  15 us
    unnamed x2, waiting for transfers between devices  11.9 us
    ppermute x2, starting transfers between devices, extended(): after = lax.ppermute(initial, axis, down)  11.5 us
  transfers between devices with their start and end apart: 7, of which 6 were waited for; matrix products, arithmetic and copies ran while one was open for 2% of the time, Pallas kernels for 0%

profile of v1, /device:TPU:1, one launch (start us, length us, event | category | flops | bytes accessed | tf_op | source)
XLA Modules:
  0.0 358.7 jit_solution(9468416502977244210)
XLA Ops:
  7.9 18.3 %all_to_all.15 = f32[32,1,1024]{2,1,0:T(1,128)S(1)} all-to-all(f32[32,1,1024]{2,1,0:T(1,128)S(1)} %broadcast_in_dim.10), channel_id=1, replica_groups=mesh['lat'=16,'lon'=32] {'lon'}, dimensions={0} | all-to-all | bytes 262144 | tf_op jit(solution)/shard_map/all_to_all | solution.py:19
  26.3 1.6 stack.39
  27.9 15.0 %all-to-all-start.1 = ((f32[16,32,1024]{2,1,0:T(8,128)}), f32[16,32,1024]{2,1,0:T(8,128)S(1)}, u32[]{:S(2)}, u32[]{:S(2)}) async-start(f32[16,32,1024]{2,1,0:T(8,128)} %stack.39), calls=%async_computation.1 | async-start | bytes 4194304 | tf_op jit(solution)/shard_map/all_to_all | solution.py:119
  44.9 93.8 %all-to-all-done.1 = f32[16,32,1024]{2,1,0:T(8,128)S(1)} async-done(((f32[16,32,1024]{2,1,0:T(8,128)}), f32[16,32,1024]{2,1,0:T(8,128)S(1)}, u32[]{:S(2)}, u32[]{:S(2)}) %all-to-all-start.1) | async-done | bytes 2097184 | tf_op jit(solution)/shard_map/all_to_all | solution.py:119
  138.7 1.3 fusion.51
  139.9 1.2 copy.89
  141.1 1.1 copy.105
  143.1 1.1 copy.100
  148.5 1.4 convolution_bitcast_fusion.1
  151.4 1.6 convolution_bitcast_fusion
  157.0 1.9 collective-permute-start
  158.9 9.4 %collective-permute-start.1 = (f32[2,1,32,512]{3,2,1,0:T(8,128)S(1)}, f32[2,1,32,512]{3,2,1,0:T(8,128)S(1)}, u32[]{:S(2)}, u32[]{:S(2)}) collective-permute-start(f32[2,1,32,512]{3,2,1,0:T(8,128)S(1)} %get-tuple-element.26), channel_id=1, source_target_pairs={{32,0},{64,32},{96,64},{128,96},{160,128},{192,160},{224,192},{256... | collective-permute-start | bytes 393224 | tf_op jit(solution)/shard_map/ppermute | solution.py:34
  169.1 1.1 collective-permute-done.1
  170.3 4.4 %collective-permute-start.2 = (f32[2,6,1,512]{3,2,1,0:T(1,128)S(1)}, f32[2,6,1,512]{3,2,1,0:T(1,128)S(1)}, u32[]{:S(2)}, u32[]{:S(2)}) collective-permute-start(f32[2,6,1,512]{3,2,1,0:T(1,128)S(1)} %get-tuple-element.23), channel_id=1, source_target_pairs={{0,1},{1,2},{2,3},{3,4},{4,5},{5,6},{6,7},{7,8},{8,9},{9,10},{10,1... | collective-permute-start | bytes 73736 | tf_op jit(solution)/shard_map/ppermute | solution.py:33
  174.7 2.1 collective-permute-start.3
  176.8 3.3 collective-permute-done.3
  182.5 2.0 fusion
  188.5 1.9 fusion.1
  193.9 1.9 copy.154
  196.2 123.1 %psum.7 = f32[9,512]{1,0:T(8,128)S(1)} all-reduce(f32[9,512]{1,0:T(8,128)S(1)} %stack.51), channel_id=1, replica_groups=mesh['lat'=16,'lon'=32] {'lat','lon'}, use_global_device_ids=true, to_apply=%region_24.25 | all-reduce | flops 4608 | bytes 36864 | tf_op jit(solution)/shard_map/psum | solution.py:159
  322.7 11.9 %reduce-scatter.4.cloned.1.call-done = f32[32,1024]{1,0:T(8,128)} async-done(((f32[512,1024]{1,0:T(8,128)}), f32[32,1024]{1,0:T(8,128)}) %reduce-scatter.4.cloned.1.call-update) | async-done | bytes 131088
  334.6 1.1 copy.155
  336.5 6.2 %all-to-all-start.2 = ((f32[32,1,1024]{2,1,0:T(1,128)}), f32[32,1,1024]{2,1,0:T(1,128)S(1)}, u32[]{:S(2)}, u32[]{:S(2)}) async-start(f32[32,1,1024]{2,1,0:T(1,128)} %copy.133), calls=%async_computation.2 | async-start | bytes 262144 | tf_op jit(solution)/shard_map/all_to_all | solution.py:47
  344.7 6.5 %all-to-all-done.2 = f32[32,1,1024]{2,1,0:T(1,128)S(1)} async-done(((f32[32,1,1024]{2,1,0:T(1,128)}), f32[32,1,1024]{2,1,0:T(1,128)S(1)}, u32[]{:S(2)}, u32[]{:S(2)}) %all-to-all-start.2) | async-done | bytes 131104 | tf_op jit(solution)/shard_map/all_to_all | solution.py:47
  (182 shorter events, 29.3 us)
Async XLA Ops:
  27.9 15.1 %copy-start.35 = (f32[4,32,512]{2,1,0:T(8,128)S(1)}, f32[4,32,512]{2,1,0:T(8,128)}, u32[]{:S(2)}) copy-start(f32[4,32,512]{2,1,0:T(8,128)} %param.5) | copy-start | bytes 786436
  27.9 16.9 %copy-start = (f32[4,32,512]{2,1,0:T(8,128)S(1)}, f32[4,32,512]{2,1,0:T(8,128)}, u32[]{:S(2)}) copy-start(f32[4,32,512]{2,1,0:T(8,128)} %param.8) | copy-start | bytes 786436
  27.9 110.8 %all-to-all-start.1 = ((f32[16,32,1024]{2,1,0:T(8,128)}), f32[16,32,1024]{2,1,0:T(8,128)S(1)}, u32[]{:S(2)}, u32[]{:S(2)}) async-start(f32[16,32,1024]{2,1,0:T(8,128)} %stack.39), calls=%async_computation.1 | async-start | bytes 4194304 | tf_op jit(solution)/shard_map/all_to_all | solution.py:119
  42.9 291.7 %reduce-scatter.4.cloned.1.call-start = ((), (), s32[]{:S(2)}) async-start(), calls=%async_computation.4 | async-start | bytes 2228224
  43.3 102.2 %copy-start.23 = (f32[128,128]{0,1:T(8,128)}, f32[128,128]{0,1:T(8,128)S(1)}, u32[]{:S(2)}) copy-start(f32[128,128]{0,1:T(8,128)S(1)} %copy.158) | copy-start | bytes 196612
  43.4 106.8 %copy-start.25 = (f32[128,128]{0,1:T(8,128)}, f32[128,128]{0,1:T(8,128)S(1)}, u32[]{:S(2)}) copy-start(f32[128,128]{0,1:T(8,128)S(1)} %copy.160) | copy-start | bytes 196612
  139.9 5.1 %copy-start.21 = (f32[512,128]{1,0:T(8,128)S(1)}, f32[512,128]{1,0:T(8,128)}, u32[]{:S(2)}) copy-start(f32[512,128]{1,0:T(8,128)} %get-tuple-element.18) | copy-start | bytes 786436
  139.9 5.2 %copy-start.20 = (f32[512,128]{1,0:T(8,128)S(1)}, f32[512,128]{1,0:T(8,128)}, u32[]{:S(2)}) copy-start(f32[512,128]{1,0:T(8,128)} %get-tuple-element.19) | copy-start | bytes 786436
  139.9 5.4 %copy-start.19 = (f32[512,128]{1,0:T(8,128)S(1)}, f32[512,128]{1,0:T(8,128)}, u32[]{:S(2)}) copy-start(f32[512,128]{1,0:T(8,128)} %get-tuple-element.20) | copy-start | bytes 786436
  142.2 8.0 %copy-start.1 = (f32[512,128]{0,1:T(8,128)}, f32[512,128]{0,1:T(8,128)S(1)}, u32[]{:S(2)}) copy-start(f32[512,128]{0,1:T(8,128)S(1)} %copy.105) | copy-start | bytes 786436
  145.5 9.5 %copy-start.36 = (f32[512,128]{0,1:T(8,128)}, f32[512,128]{0,1:T(8,128)S(1)}, u32[]{:S(2)}) copy-start(f32[512,128]{0,1:T(8,128)S(1)} %copy.91) | copy-start | bytes 786436
  154.8 13.5 %copy-start.44 = (f32[9,512]{1,0:T(8,128)S(1)}, f32[9,512]{1,0:T(8,128)}, u32[]{:S(2)}) copy-start(f32[9,512]{1,0:T(8,128)} %param.9) | copy-start | bytes 55300
  157.0 12.2 %collective-permute-start = (f32[2,1,32,512]{3,2,1,0:T(8,128)S(1)}, f32[2,1,32,512]{3,2,1,0:T(8,128)S(1)}, u32[]{:S(2)}, u32[]{:S(2)}) collective-permute-start(f32[2,1,32,512]{3,2,1,0:T(8,128)S(1)} %get-tuple-element.25), channel_id=1, source_target_pairs={{0,32},{32,64},{64,96},{96,128},{128,160},{160,192},{192,224},{224... | collective-permute-start | bytes 393224 | tf_op jit(solution)/shard_map/ppermute | solution.py:33
  158.9 11.3 %collective-permute-start.1 = (f32[2,1,32,512]{3,2,1,0:T(8,128)S(1)}, f32[2,1,32,512]{3,2,1,0:T(8,128)S(1)}, u32[]{:S(2)}, u32[]{:S(2)}) collective-permute-start(f32[2,1,32,512]{3,2,1,0:T(8,128)S(1)} %get-tuple-element.26), channel_id=1, source_target_pairs={{32,0},{64,32},{96,64},{128,96},{160,128},{192,160},{224,192},{256... | collective-permute-start | bytes 393224 | tf_op jit(solution)/shard_map/ppermute | solution.py:34
  170.3 6.6 %collective-permute-start.2 = (f32[2,6,1,512]{3,2,1,0:T(1,128)S(1)}, f32[2,6,1,512]{3,2,1,0:T(1,128)S(1)}, u32[]{:S(2)}, u32[]{:S(2)}) collective-permute-start(f32[2,6,1,512]{3,2,1,0:T(1,128)S(1)} %get-tuple-element.23), channel_id=1, source_target_pairs={{0,1},{1,2},{2,3},{3,4},{4,5},{5,6},{6,7},{7,8},{8,9},{9,10},{10,1... | collective-permute-start | bytes 73736 | tf_op jit(solution)/shard_map/ppermute | solution.py:33
  174.7 5.4 %collective-permute-start.3 = (f32[2,6,1,512]{3,2,1,0:T(1,128)S(1)}, f32[2,6,1,512]{3,2,1,0:T(1,128)S(1)}, u32[]{:S(2)}, u32[]{:S(2)}) collective-permute-start(f32[2,6,1,512]{3,2,1,0:T(1,128)S(1)} %get-tuple-element.24), channel_id=1, source_target_pairs={{1,0},{2,1},{3,2},{4,3},{5,4},{6,5},{7,6},{8,7},{9,8},{10,9},{11,1... | collective-permute-start | bytes 73736 | tf_op jit(solution)/shard_map/ppermute | solution.py:34
  181.4 6.3 %copy-start.43 = (f32[128,128]{0,1:T(8,128)}, f32[128,128]{0,1:T(8,128)S(1)}, u32[]{:S(2)}) copy-start(f32[128,128]{0,1:T(8,128)S(1)} %copy.163) | copy-start | bytes 196612
  195.8 124.9 %copy-start.2 = (f32[512,128]{0,1:T(8,128)S(1)}, f32[512,128]{0,1:T(8,128)}, u32[]{:S(2)}) copy-start(f32[512,128]{0,1:T(8,128)} %copy-done.1) | copy-start | bytes 786436
  195.8 124.9 %copy-start.14 = (f32[2,128,512]{1,2,0:T(8,128)S(1)}, f32[2,128,512]{1,2,0:T(8,128)}, u32[]{:S(2)}) copy-start(f32[2,128,512]{1,2,0:T(8,128)} %copy-done.13) | copy-start | bytes 1572868
  195.8 125.5 %copy-start.4 = (f32[512,128]{0,1:T(8,128)S(1)}, f32[512,128]{0,1:T(8,128)}, u32[]{:S(2)}) copy-start(f32[512,128]{0,1:T(8,128)} %copy-done.3) | copy-start | bytes 786436
  195.8 125.5 %copy-start.16 = (f32[2,128,512]{1,2,0:T(8,128)S(1)}, f32[2,128,512]{1,2,0:T(8,128)}, u32[]{:S(2)}) copy-start(f32[2,128,512]{1,2,0:T(8,128)} %copy-done.15) | copy-start | bytes 1572868
  195.8 126.2 %copy-start.18 = (f32[2,128,512]{1,2,0:T(8,128)S(1)}, f32[2,128,512]{1,2,0:T(8,128)}, u32[]{:S(2)}) copy-start(f32[2,128,512]{1,2,0:T(8,128)} %copy-done.17) | copy-start | bytes 1572868
  321.2 21.5 %copy-start.12 = (f32[2,128,512]{1,2,0:T(8,128)S(1)}, f32[2,128,512]{1,2,0:T(8,128)}, u32[]{:S(2)}) copy-start(f32[2,128,512]{1,2,0:T(8,128)} %copy-done.11) | copy-start | bytes 1572868
  336.5 14.7 %all-to-all-start.2 = ((f32[32,1,1024]{2,1,0:T(1,128)}), f32[32,1,1024]{2,1,0:T(1,128)S(1)}, u32[]{:S(2)}, u32[]{:S(2)}) async-start(f32[32,1,1024]{2,1,0:T(1,128)} %copy.133), calls=%async_computation.2 | async-start | bytes 262144 | tf_op jit(solution)/shard_map/all_to_all | solution.py:47
  (28 other events, 64.3 us)
Sparse Core Ops, SparseCore 0:
  195.9 138.6 reduce-scatter.3
